TPU v7x, 32 devices: a whole 2x2x4 slice. The times are simulated.
32 devices in a mesh: dp: 8 (over z, y), mp: 4 (over x, core).
Axes of the slice: x: 2, y: 2, z: 4, core: 2. Of those that a mesh axis runs over, the one named last changes fastest.
Arguments:
- tokens: bfloat16 [16384, 768], P('dp'), may hold values from -6 to 6
- lengths: int32 [8, 2], P('dp'), may hold values from 0 to 2048, as said below
- mix_gain: float32 [768], replicated, may hold values from 0.5 to 1.5
- mix_shift: float32 [768], replicated, may hold values from -4 to 4
- proj_in: bfloat16 [768, 3, 768], P(None, None, 'mp'), may hold values from -0.21875 to 0.21875
- bias_in: float32 [3, 768], P(None, 'mp'), may hold values from -4 to 4
- short_taps: float32 [3, 3, 768], P(None, None, 'mp'), may hold values from -6 to 6
- long_taps: bfloat16 [2048, 768], P('dp', 'mp'), may hold values from -0.75 to 0.75
- decay_rates: float32 [768], P('mp'), may hold values from 0.00024414062 to 0.05
- skip_gain: float32 [768], P('mp'), may hold values from -6 to 6
- proj_out: bfloat16 [768, 768], P('mp'), may hold values from -0.21875 to 0.21875
- bias_out: float32 [768], replicated, may hold values from -4 to 4
- mlp_gain: float32 [768], replicated, may hold values from 0.5 to 1.5
- mlp_shift: float32 [768], replicated, may hold values from -4 to 4
- proj_up: bfloat16 [768, 3072], P(None, 'mp'), may hold values from -0.21875 to 0.21875
- bias_up: float32 [3072], P('mp'), may hold values from -4 to 4
- proj_down: bfloat16 [3072, 768], P('mp'), may hold values from -0.109375 to 0.109375
- bias_down: float32 [768], replicated, may hold values from -4 to 4
- cotangent: bfloat16 [16384, 768], P('dp'), may hold values from -6 to 6
Outputs:
- output: bfloat16 [16384, 768], P('dp')
- input_grad: float32 [16384, 768], P('dp')
- grad_mix_gain: float32 [768], replicated
- grad_mix_shift: float32 [768], replicated
- grad_proj_in: float32 [768, 3, 768], P(None, None, 'mp')
- grad_bias_in: float32 [3, 768], P(None, 'mp')
- grad_short_taps: float32 [3, 3, 768], P(None, None, 'mp')
- grad_long_taps: float32 [2048, 768], P('dp', 'mp')
- grad_decay_rates: float32 [768], P('mp')
- grad_skip_gain: float32 [768], P('mp')
- grad_proj_out: float32 [768, 768], P('mp')
- grad_bias_out: float32 [768], replicated
- grad_mlp_gain: float32 [768], replicated
- grad_mlp_shift: float32 [768], replicated
- grad_proj_up: float32 [768, 3072], P(None, 'mp')
- grad_bias_up: float32 [3072], P('mp')
- grad_proj_down: float32 [3072, 768], P('mp')
- grad_bias_down: float32 [768], replicated
Inputs may be any that keep to these rules, and one draw needn't show every extreme that they name: Row g gives the lengths of the documents packed in order into group g's 2048 tokens: either one document of 2048 tokens and 0, or two of half of 2048 each; exactly half of the rows hold two documents.
All inputs are finite; a program needn't handle non-finite values.
Results may differ from a plain program's by a relative error of at most 0.024.
Values may be sent and summed in bfloat16 or wider, within the bound.
No kernel may reach another device: no remote copies, remote signals or barrier semaphores. Data moves between devices by JAX's collectives and lax.ppermute only.
A program may use at most 256 MiB of HBM per device.

v0:
```python
from functools import partial
import math
import jax
import jax.numpy as jnp
from jax import lax
from jax.sharding import PartitionSpec as P


def layer_norm(values, scale_vec, shift_vec):
    average = jnp.mean(values, axis=-1, keepdims=True)
    centered = values - average
    variance = jnp.mean(centered * centered, axis=-1, keepdims=True)
    return centered * lax.rsqrt(variance + 1e-05) * scale_vec + shift_vec


def short_mix(first_len, streams, short_taps):
    seq_len = streams.shape[0]
    positions = jnp.arange(seq_len, dtype=jnp.int32)[:, None, None]
    result = short_taps[0] * streams
    for offset in (1, 2):
        shifted = jnp.concatenate(
            [jnp.zeros((offset,) + streams.shape[1:], streams.dtype), streams[:-offset]], axis=0
        )
        valid_mask = (positions >= offset) & (
            (positions < first_len) | (positions - offset >= first_len)
        )
        result = result + valid_mask.astype(streams.dtype) * (short_taps[offset] * shifted)
    return (result[:, 0], result[:, 1] * result[:, 2])


def build_kernel(raw_taps, decay_rates):
    seq_len = raw_taps.shape[0]
    positions = jnp.arange(seq_len).astype(raw_taps.dtype)[:, None]
    decayed = raw_taps * jnp.exp(-decay_rates * positions)
    padded = jnp.pad(decayed, ((1, 1), (0, 0)))
    pooled = (padded[:-2] + padded[1:-1] + padded[2:]) / 3.0
    return jnp.sign(pooled) * jnp.maximum(jnp.abs(pooled) - 0.003, 0.0)


def gate_mix(queries, conv_out, mixed_in, skip_gain):
    return queries * (conv_out + skip_gain * mixed_in)


def gelu_exact(values):
    return jax.nn.gelu(values, approximate=False)


def plain_product(lhs_mat, rhs_mat):
    return jnp.dot(lhs_mat, rhs_mat, preferred_element_type=jnp.float32)


def tall_product(lhs_mat, rhs_mat):
    return lax.dot_general(
        lhs_mat, rhs_mat, (((0,), (0,)), ((), ())), preferred_element_type=jnp.float32
    )


def wide_product(lhs_mat, rhs_mat):
    return lax.dot_general(
        lhs_mat, rhs_mat, (((1,), (1,)), ((), ())), preferred_element_type=jnp.float32
    )


def exact_product(lhs_mat, rhs_mat):
    return jnp.dot(
        lhs_mat, rhs_mat, precision=lax.Precision.HIGHEST, preferred_element_type=jnp.float32
    )


def across(table, values):
    return jnp.einsum(
        "jn,knc->kjc",
        table,
        values,
        precision=lax.Precision.HIGHEST,
        preferred_element_type=jnp.float32,
    )


def dft_pair(out_count, in_count, period):
    outer = lax.iota(jnp.int32, out_count)[:, None]
    inner = lax.iota(jnp.int32, in_count)[None, :]
    angles = (outer * inner % period).astype(jnp.float32) * (2.0 * math.pi / period)
    return (jnp.cos(angles), jnp.sin(angles))


def twiddles(rows_p, cols_q, period):
    outer = lax.iota(jnp.int32, rows_p)[:, None]
    inner = lax.iota(jnp.int32, cols_q)[None, :]
    angles = (outer * inner % period).astype(jnp.float32) * (2.0 * math.pi / period)
    return (jnp.cos(angles)[:, :, None], jnp.sin(angles)[:, :, None])


def split_sizes(seq_len):
    period = 2 * seq_len
    exponent = period.bit_length() - 1
    rows_p = 2 ** ((exponent + 1) // 2)
    return (period, rows_p, period // rows_p)


def spectrum(signal):
    seq_len, columns = signal.shape
    period, rows_p, cols_q = split_sizes(seq_len)
    half = rows_p // 2
    flat = signal.reshape(half, cols_q * columns)
    cos_p, sin_p = dft_pair(rows_p, half, rows_p)
    first_re = exact_product(cos_p, flat).reshape(rows_p, cols_q, columns)
    first_im = -exact_product(sin_p, flat).reshape(rows_p, cols_q, columns)
    turn_cos, turn_sin = twiddles(rows_p, cols_q, period)
    turned_re = first_re * turn_cos + first_im * turn_sin
    turned_im = first_im * turn_cos - first_re * turn_sin
    cos_q, sin_q = dft_pair(cols_q, cols_q, cols_q)
    spec_re = across(cos_q, turned_re) + across(sin_q, turned_im)
    spec_im = across(cos_q, turned_im) - across(sin_q, turned_re)
    return (spec_re, spec_im)


def inverse_real(spec_re, spec_im):
    rows_p, cols_q, columns = spec_re.shape
    period = rows_p * cols_q
    half = rows_p // 2
    cos_q, sin_q = dft_pair(cols_q, cols_q, cols_q)
    back_re = across(cos_q, spec_re) - across(sin_q, spec_im)
    back_im = across(cos_q, spec_im) + across(sin_q, spec_re)
    turn_cos, turn_sin = twiddles(rows_p, cols_q, period)
    turned_re = back_re * turn_cos - back_im * turn_sin
    turned_im = back_im * turn_cos + back_re * turn_sin
    cos_i, sin_i = dft_pair(half, rows_p, rows_p)
    result = exact_product(cos_i, turned_re.reshape(rows_p, cols_q * columns)) - exact_product(
        sin_i, turned_im.reshape(rows_p, cols_q * columns)
    )
    return result.reshape(half * cols_q, columns) / float(period)


def long_conv(mixed_in, kernel, mask_one, mask_two):
    channels = mixed_in.shape[1]
    stacked = jnp.concatenate([mask_one * mixed_in, mask_two * mixed_in, kernel], axis=1)
    spec_re, spec_im = spectrum(stacked)
    sig_re = spec_re[:, :, : 2 * channels]
    sig_im = spec_im[:, :, : 2 * channels]
    ker_re = jnp.tile(spec_re[:, :, 2 * channels :], (1, 1, 2))
    ker_im = jnp.tile(spec_im[:, :, 2 * channels :], (1, 1, 2))
    prod_re = sig_re * ker_re - sig_im * ker_im
    prod_im = sig_re * ker_im + sig_im * ker_re
    totals = inverse_real(prod_re, prod_im)
    return mask_one * totals[:, :channels] + mask_two * totals[:, channels:]


def long_conv_back(grad_conv, mixed_in, kernel, mask_one, mask_two):
    channels = mixed_in.shape[1]
    stacked = jnp.concatenate(
        [
            mask_one * mixed_in,
            mask_two * mixed_in,
            mask_one * grad_conv,
            mask_two * grad_conv,
            kernel,
        ],
        axis=1,
    )
    spec_re, spec_im = spectrum(stacked)
    sig_re = spec_re[:, :, : 2 * channels]
    sig_im = spec_im[:, :, : 2 * channels]
    out_re = spec_re[:, :, 2 * channels : 4 * channels]
    out_im = spec_im[:, :, 2 * channels : 4 * channels]
    ker_re = jnp.tile(spec_re[:, :, 4 * channels :], (1, 1, 2))
    ker_im = jnp.tile(spec_im[:, :, 4 * channels :], (1, 1, 2))
    back_in_re = ker_re * out_re + ker_im * out_im
    back_in_im = ker_re * out_im - ker_im * out_re
    cor_re = sig_re * out_re + sig_im * out_im
    cor_im = sig_re * out_im - sig_im * out_re
    cor_re = cor_re[:, :, :channels] + cor_re[:, :, channels:]
    cor_im = cor_im[:, :, :channels] + cor_im[:, :, channels:]
    totals = inverse_real(
        jnp.concatenate([back_in_re, cor_re], axis=2), jnp.concatenate([back_in_im, cor_im], axis=2)
    )
    grad_mixed = mask_one * totals[:, :channels] + mask_two * totals[:, channels : 2 * channels]
    return (grad_mixed, totals[:, 2 * channels :])


def per_device(
    tokens,
    lengths,
    mix_gain,
    mix_shift,
    proj_in,
    bias_in,
    short_taps,
    long_taps,
    decay_rates,
    skip_gain,
    proj_out,
    bias_out,
    mlp_gain,
    mlp_shift,
    proj_up,
    bias_up,
    proj_down,
    bias_down,
    cotangent,
):
    seq_len, width = tokens.shape
    channels = proj_in.shape[2]
    first_len = lengths[0, 0]
    second_len = lengths[0, 1]
    positions = jnp.arange(seq_len, dtype=jnp.int32)[:, None]
    mask_one = (positions < first_len).astype(jnp.float32)
    mask_two = ((positions >= first_len) & (positions < first_len + second_len)).astype(jnp.float32)
    tokens_f = tokens.astype(jnp.float32)
    normed, norm_pull = jax.vjp(layer_norm, tokens_f, mix_gain, mix_shift)
    normed_low = normed.astype(jnp.bfloat16)
    proj_flat = proj_in.reshape(width, 3 * channels)
    streams = (plain_product(normed_low, proj_flat) + bias_in.reshape(-1)).reshape(
        seq_len, 3, channels
    )
    (queries, mixed_in), short_pull = jax.vjp(partial(short_mix, first_len), streams, short_taps)
    gathered = lax.all_gather(long_taps, "dp", axis=0, tiled=True)
    kernel, kernel_pull = jax.vjp(build_kernel, gathered.astype(jnp.float32), decay_rates)
    conv_out = long_conv(mixed_in, kernel, mask_one, mask_two)
    gated_out, gate_pull = jax.vjp(gate_mix, queries, conv_out, mixed_in, skip_gain)
    gated_low = gated_out.astype(jnp.bfloat16)
    attn_terms = plain_product(gated_low, proj_out)
    attn_out = lax.psum(attn_terms.astype(jnp.bfloat16), "mp").astype(jnp.float32) + bias_out
    hidden_one = tokens_f + attn_out
    normed_two, norm_two_pull = jax.vjp(layer_norm, hidden_one, mlp_gain, mlp_shift)
    normed_two_low = normed_two.astype(jnp.bfloat16)
    pre_act = plain_product(normed_two_low, proj_up) + bias_up
    hidden, gelu_pull = jax.vjp(gelu_exact, pre_act)
    hidden_low = hidden.astype(jnp.bfloat16)
    down_terms = plain_product(hidden_low, proj_down)
    mlp_out = lax.psum(down_terms.astype(jnp.bfloat16), "mp").astype(jnp.float32) + bias_down
    output = (hidden_one + mlp_out).astype(jnp.bfloat16)
    grad_proj_down = tall_product(hidden_low, cotangent)
    grad_bias_down = jnp.sum(cotangent.astype(jnp.float32), axis=0)
    (grad_pre,) = gelu_pull(wide_product(cotangent, proj_down))
    grad_pre_low = grad_pre.astype(jnp.bfloat16)
    grad_proj_up = tall_product(normed_two_low, grad_pre_low)
    grad_bias_up = jnp.sum(grad_pre_low.astype(jnp.float32), axis=0)
    grad_norm_terms = wide_product(grad_pre_low, proj_up)
    cot_f = cotangent.astype(jnp.float32)
    grad_normed_two = lax.psum(grad_norm_terms.astype(jnp.bfloat16), "mp").astype(jnp.float32)
    grad_hidden_part, grad_mlp_gain, grad_mlp_shift = norm_two_pull(grad_normed_two)
    grad_hidden_one = cot_f + grad_hidden_part
    grad_bias_out = jnp.sum(grad_hidden_one, axis=0)
    grad_attn_low = grad_hidden_one.astype(jnp.bfloat16)
    grad_proj_out = tall_product(gated_low, grad_attn_low)
    grad_gated = wide_product(grad_attn_low, proj_out)
    grad_queries, grad_conv, grad_mixed_direct, grad_skip_gain = gate_pull(grad_gated)
    regathered = lax.all_gather(long_taps, "dp", axis=0, tiled=True)
    kernel_back, kernel_pull_back = jax.vjp(
        build_kernel, regathered.astype(jnp.float32), decay_rates
    )
    grad_mixed_conv, grad_kernel = long_conv_back(
        grad_conv, mixed_in, kernel_back, mask_one, mask_two
    )
    grad_taps_full, grad_decay_rates = kernel_pull_back(grad_kernel)
    grad_streams, grad_short_taps = short_pull((grad_queries, grad_mixed_direct + grad_mixed_conv))
    grad_streams_low = grad_streams.reshape(seq_len, 3 * channels).astype(jnp.bfloat16)
    grad_proj_in = tall_product(normed_low, grad_streams_low).reshape(width, 3, channels)
    grad_bias_in = jnp.sum(grad_streams_low.astype(jnp.float32), axis=0).reshape(3, channels)
    grad_normed = lax.psum(
        wide_product(grad_streams_low, proj_flat).astype(jnp.bfloat16), "mp"
    ).astype(jnp.float32)
    grad_tokens_part, grad_mix_gain, grad_mix_shift = norm_pull(grad_normed)
    input_grad = grad_hidden_one + grad_tokens_part
    grad_long_taps = lax.psum_scatter(
        grad_taps_full.astype(jnp.bfloat16), "dp", scatter_dimension=0, tiled=True
    ).astype(jnp.float32)
    (
        grad_mix_gain,
        grad_mix_shift,
        grad_proj_in,
        grad_bias_in,
        grad_short_taps,
        grad_decay_rates,
        grad_skip_gain,
        grad_proj_out,
        grad_bias_out,
        grad_mlp_gain,
        grad_mlp_shift,
        grad_proj_up,
        grad_bias_up,
        grad_proj_down,
        grad_bias_down,
    ) = (
        lax.psum(grad_mix_gain.astype(jnp.bfloat16), "dp").astype(jnp.float32),
        lax.psum(grad_mix_shift.astype(jnp.bfloat16), "dp").astype(jnp.float32),
        lax.psum(grad_proj_in.astype(jnp.bfloat16), "dp").astype(jnp.float32),
        lax.psum(grad_bias_in.astype(jnp.bfloat16), "dp").astype(jnp.float32),
        lax.psum(grad_short_taps.astype(jnp.bfloat16), "dp").astype(jnp.float32),
        lax.psum(grad_decay_rates.astype(jnp.bfloat16), "dp").astype(jnp.float32),
        lax.psum(grad_skip_gain.astype(jnp.bfloat16), "dp").astype(jnp.float32),
        lax.psum(grad_proj_out.astype(jnp.bfloat16), "dp").astype(jnp.float32),
        lax.psum(grad_bias_out.astype(jnp.bfloat16), "dp").astype(jnp.float32),
        lax.psum(grad_mlp_gain.astype(jnp.bfloat16), "dp").astype(jnp.float32),
        lax.psum(grad_mlp_shift.astype(jnp.bfloat16), "dp").astype(jnp.float32),
        lax.psum(grad_proj_up.astype(jnp.bfloat16), "dp").astype(jnp.float32),
        lax.psum(grad_bias_up.astype(jnp.bfloat16), "dp").astype(jnp.float32),
        lax.psum(grad_proj_down.astype(jnp.bfloat16), "dp").astype(jnp.float32),
        lax.psum(grad_bias_down.astype(jnp.bfloat16), "dp").astype(jnp.float32),
    )
    return (
        output,
        input_grad,
        grad_mix_gain,
        grad_mix_shift,
        grad_proj_in,
        grad_bias_in,
        grad_short_taps,
        grad_long_taps,
        grad_decay_rates,
        grad_skip_gain,
        grad_proj_out,
        grad_bias_out,
        grad_mlp_gain,
        grad_mlp_shift,
        grad_proj_up,
        grad_bias_up,
        grad_proj_down,
        grad_bias_down,
    )


def solution(mesh):
    in_specs = (
        P("dp", None),
        P("dp", None),
        P(),
        P(),
        P(None, None, "mp"),
        P(None, "mp"),
        P(None, None, "mp"),
        P("dp", "mp"),
        P("mp"),
        P("mp"),
        P("mp", None),
        P(),
        P(),
        P(),
        P(None, "mp"),
        P("mp"),
        P("mp", None),
        P(),
        P("dp", None),
    )
    out_specs = (
        P("dp", None),
        P("dp", None),
        P(),
        P(),
        P(None, None, "mp"),
        P(None, "mp"),
        P(None, None, "mp"),
        P("dp", "mp"),
        P("mp"),
        P("mp"),
        P("mp", None),
        P(),
        P(),
        P(),
        P(None, "mp"),
        P("mp"),
        P("mp", None),
        P(),
    )
    return jax.shard_map(
        per_device, mesh=mesh, in_specs=in_specs, out_specs=out_specs, check_vma=False
    )
```

profile of v0, /device:TPU:0, one launch (start us, length us, event | category | flops | bytes accessed | tf_op | source)
XLA Modules:
  0.0 1298.6 jit_solution(12647565833582045572)
XLA Ops:
  19.3 33.9 %all_gather.4 = bf16[2048,192]{0,1:T(8,128)(2,1)S(1)} all-gather(bf16[256,192]{0,1:T(8,128)(2,1)S(1)} %copy-done.53), channel_id=1, replica_groups=mesh['dp'=8,'mp'=4] {'dp'}, dimensions={0}, use_global_device_ids=true | all-gather | bytes 884736 | tf_op jit(solution)/shard_map/all_gather | solution.py:217
  69.1 5.8 copy.51
  74.9 6.4 reshape.291
  81.2 6.4 dot_general.122
  87.6 16.4 %fusion.51 = f32[64,64,576]{2,0,1:T(8,128)} fusion(f32[64,576,32]{1,0,2:T(8,128)} %dot_general.122), kind=kOutput, calls=%fused_computation.95 | convolution fusion | flops 905998336 | bytes 14155776 | tf_op jit(solution)/shard_map/dot_general | solution.py:65
  104.1 20.2 %multiply_add_fusion.1 = (f32[64,64,576]{2,0,1:T(8,128)}, f32[64,64,576]{2,0,1:T(8,128)S(1)}) fusion(f32[64,64,576]{2,0,1:T(8,128)} %fusion.51, f32[64,64]{0,1:T(8,128)S(1)} %copy.55, f32[64,64]{0,1:T(8,128)S(1)} %copy.53, f32[64,576,32]{1,0,2:T(8,128)} %dot_general.122), kind=kOutput, calls=%fused_computation.23 | convolution fusion | flops 922513408 | bytes 33062912 | tf_op jit(solution)/shard_map/dot_general | solution.py:65
  124.3 21.2 %fusion.10 = f32[64,576,64]{1,2,0:T(8,128)} fusion(f32[64,64,576]{2,0,1:T(8,128)S(1)} %get-tuple-element.76), kind=kOutput, calls=%fused_computation.24 | convolution fusion | flops 1811996672 | bytes 18874368 | tf_op jit(solution)/shard_map/jn,knc->kjc/dot_general | solution.py:71
  145.5 21.2 %fusion.12 = f32[64,576,64]{1,2,0:T(8,128)} fusion(f32[64,64,576]{2,0,1:T(8,128)S(1)} %get-tuple-element.76), kind=kOutput, calls=%fused_computation.26 | convolution fusion | flops 1811996672 | bytes 18874368 | tf_op jit(solution)/shard_map/jn,knc->kjc/dot_general | solution.py:71
  166.7 23.6 %subtract_bitcast_fusion.2 = f32[64,64,576]{2,1,0:T(8,128)} fusion(f32[64,576,64]{1,2,0:T(8,128)} %fusion.10, f32[64,64,576]{2,0,1:T(8,128)} %get-tuple-element.75), kind=kOutput, calls=%fused_computation.20 | convolution fusion | flops 1814355968 | bytes 28311552 | tf_op jit(solution)/shard_map/jn,knc->kjc/dot_general | solution.py:71
  190.3 22.4 %add_bitcast_fusion.2 = f32[64,64,576]{2,1,0:T(8,128)S(1)} fusion(f32[64,576,64]{1,2,0:T(8,128)} %fusion.12, f32[64,64,576]{2,0,1:T(8,128)} %get-tuple-element.75), kind=kOutput, calls=%fused_computation.21 | convolution fusion | flops 1814355968 | bytes 28311552 | tf_op jit(solution)/shard_map/jn,knc->kjc/dot_general | solution.py:71
  217.0 4.5 tile.16
  221.5 10.7 tile.17
  234.4 4.4 tile.18
  238.8 11.1 tile.19
  249.9 9.6 multiply_subtract_fusion.5
  259.6 7.9 fusion.93
  267.4 7.8 fusion.105
  275.2 7.9 fusion.95
  283.1 14.9 %multiply_add_fusion.4 = (f32[64,384,64]{1,2,0:T(8,128)}, f32[64,384,64]{1,2,0:T(8,128)}) fusion(f32[64,64]{1,0:T(8,128)S(1)} %get-tuple-element.98, f32[64,64]{1,0:T(8,128)S(1)} %get-tuple-element.99, f32[64,384,64]{1,2,0:T(8,128)} %fusion.93, f32[64,384,64]{1,2,0:T(8,128)} %fusion.105, f32[64,384,64]{1,2,0:T(8,128)} %fusion.95, ...), kind=kOutput, calls=%fused_computation.90 | convolution fusion | flops 1220599808 | bytes 37781504 | tf_op jit(solution)/shard_map/jn,knc->kjc/dot_general | solution.py:71
  298.0 6.5 copy.80
  311.7 5.5 fusion.1
  320.4 4.9 fusion.291
  338.8 69.5 %all-reduce.22.cloned.1.call-done = bf16[2048,768]{1,0:T(8,128)(2,1)} async-done(((bf16[2048,768]{1,0:T(8,128)(2,1)}), bf16[2048,768]{1,0:T(8,128)(2,1)}) %all-reduce.22.cloned.1.call-update) | async-done | bytes 3145744 | tf_op jit(solution)/shard_map/psum | solution.py:223
  419.0 19.1 %fusion.283 = (bf16[768]{0:T(1024)(128)(2,1)}, bf16[2048,768]{1,0:T(8,128)(2,1)S(1)}, f32[2048,768]{1,0:T(8,128)}) fusion(f32[2048,768]{1,0:T(8,128)S(1)} %fusion.278, f32[768]{0:T(1024)S(1)} %copy-done.82, bf16[2048,768]{1,0:T(8,128)(2,1)S(1)} %copy-done.24, bf16[768,768]{1,0:T(8,128)(2,1)S(1)} %copy-done), kind=kOutput, calls=%fused_computation.369 | convolution fusion | flops 2532310272 | bytes 20058624 | tf_op jit(solution)/shard_map/dot_general | solution.py:59
  443.8 5.5 multiply_convert_fusion
  455.4 57.0 %all-reduce.24.cloned.1.call-done = bf16[2048,768]{1,0:T(8,128)(2,1)} async-done(((bf16[2048,768]{1,0:T(8,128)(2,1)}), bf16[2048,768]{1,0:T(8,128)(2,1)}) %all-reduce.24.cloned.1.call-update) | async-done | bytes 3145744 | tf_op jit(solution)/shard_map/psum | solution.py:241
  512.4 5.6 fusion.40
  518.9 5.2 fusion.41
  528.5 5.6 multiply_reduce_fusion.4
  538.9 9.2 copy.62
  548.1 9.1 reshape.294
  557.1 8.9 dot_general.142
  566.0 25.4 %fusion.30 = f32[64,64,960]{2,0,1:T(8,128)} fusion(f32[64,960,32]{1,0,2:T(8,128)} %dot_general.142), kind=kOutput, calls=%fused_computation.46 | convolution fusion | flops 1509978112 | bytes 23592960 | tf_op jit(solution)/shard_map/dot_general | solution.py:65
  591.4 26.6 %multiply_add_fusion = (f32[64,64,960]{2,0,1:T(8,128)}, f32[64,64,960]{2,0,1:T(8,128)}) fusion(f32[64,64,960]{2,0,1:T(8,128)} %fusion.30, f32[64,64]{0,1:T(8,128)S(1)} %copy-done.40, f32[64,64]{0,1:T(8,128)S(1)} %copy-done.42, f32[64,960,32]{1,0,2:T(8,128)S(1)} %copy-done.10), kind=kOutput, calls=%fused_computation.7 | convolution fusion | flops 1537503232 | bytes 55083008 | tf_op jit(solution)/shard_map/dot_general | solution.py:65
  618.0 36.1 %fusion.2 = f32[64,960,64]{1,2,0:T(8,128)} fusion(f32[64,64,960]{2,0,1:T(8,128)} %get-tuple-element.68), kind=kOutput, calls=%fused_computation.8 | convolution fusion | flops 3019956224 | bytes 31457280 | tf_op jit(solution)/shard_map/jn,knc->kjc/dot_general | solution.py:71
  654.1 36.5 %fusion.4 = f32[64,960,64]{1,2,0:T(8,128)} fusion(f32[64,64,960]{2,0,1:T(8,128)} %get-tuple-element.68), kind=kOutput, calls=%fused_computation.10 | convolution fusion | flops 3019956224 | bytes 31457280 | tf_op jit(solution)/shard_map/jn,knc->kjc/dot_general | solution.py:71
  690.6 32.7 %subtract_bitcast_fusion = f32[64,64,960]{2,1,0:T(8,128)} fusion(f32[64,960,64]{1,2,0:T(8,128)} %fusion.2, f32[64,64,960]{2,0,1:T(8,128)} %get-tuple-element.67), kind=kOutput, calls=%fused_computation.4 | convolution fusion | flops 3023888384 | bytes 47185920 | tf_op jit(solution)/shard_map/jn,knc->kjc/dot_general | solution.py:71
  723.3 32.6 %add_bitcast_fusion = f32[64,64,960]{2,1,0:T(8,128)} fusion(f32[64,960,64]{1,2,0:T(8,128)} %fusion.4, f32[64,64,960]{2,0,1:T(8,128)} %get-tuple-element.67), kind=kOutput, calls=%fused_computation.5 | convolution fusion | flops 3023888384 | bytes 47185920 | tf_op jit(solution)/shard_map/jn,knc->kjc/dot_general | solution.py:71
  758.1 4.5 tile.40
  762.6 10.7 tile.41
  775.5 4.4 tile.42
  780.0 10.7 tile.43
  790.7 23.6 %multiply_add_fusion.3 = (f32[64,64,384]{2,1,0:T(8,128)}, f32[64,64,384]{2,1,0:T(8,128)}, f32[64,64,384]{2,1,0:T(8,128)}, f32[64,64,384]{2,1,0:T(8,128)}) fusion(f32[64,64,384]{2,1,0:T(8,128)} %tile.43, f32[64,64,384]{2,1,0:T(8,128)} %tile.41, f32[64,64,960]{2,1,0:T(8,128)} %subtract_bitcast_fusion, f32[64,64,960]{2,1,0:T(8,128)} %add_bitcast_fusion), kind=kLoop, calls=%fused_computation.71 | loop fusion | flops 18874368 | bytes 62914560 | tf_op jit(solution)/shard_map/add | solution.py:168
  814.3 4.7 slice_add_fusion
  819.5 12.4 fusion.26
  831.9 12.7 fusion.27
  844.6 4.6 slice_add_fusion.1
  851.2 12.4 fusion.28
  863.6 28.0 %add_bitcast_fusion.1 = (f32[64,64,576]{2,1,0:T(8,128)}, f32[64,64,576]{2,1,0:T(8,128)}) fusion(f32[64,64]{1,0:T(8,128)S(1)} %copy-done.36, f32[64,64]{1,0:T(8,128)S(1)} %copy-done.38, f32[64,576,64]{1,2,0:T(8,128)} %fusion.26, f32[64,576,64]{1,2,0:T(8,128)} %fusion.28, f32[64,576,64]{1,2,0:T(8,128)} %fusion.27, f32[64,64,192]{2,1,0:T(8,128)} %copy-done.16, ...), kind=kOutput, calls=%fused_computation.18 | convolution fusion | flops 1833230336 | bytes 56655872 | tf_op jit(solution)/shard_map/jn,knc->kjc/dot_general | solution.py:71
  891.6 11.9 reshape.296
  903.5 11.9 reshape.295
  915.5 7.7 fusion.160
  923.1 6.8 fusion
  929.9 6.6 div.72
  936.5 6.6 fusion.290
  961.0 5.3 multiply_reduce_fusion.3
  975.0 6.7 convolution_convert_fusion.3
  981.8 7.5 convolution_convert_fusion.4
  999.6 14.3 %reduce-scatter.2.cloned.1.call-done = bf16[256,192]{0,1:T(8,128)(2,1)} async-done(((bf16[2048,192]{0,1:T(8,128)(2,1)}), bf16[256,192]{0,1:T(8,128)(2,1)}) %reduce-scatter.2.cloned.1.call-update) | async-done | bytes 98320 | tf_op jit(solution)/shard_map/reduce_scatter | solution.py:266
  1015.5 120.2 %all-reduce.28.cloned.1.call-done = (bf16[2048,768]{1,0:T(8,128)(2,1)}, bf16[2048,768]{1,0:T(8,128)(2,1)}) async-done(((bf16[2048,768]{1,0:T(8,128)(2,1)}, bf16[2048,768]{1,0:T(8,128)(2,1)}), (bf16[2048,768]{1,0:T(8,128)(2,1)}, bf16[2048,768]{1,0:T(8,128)(2,1)})) %all-reduce.28.cloned.1.call-update) | async-done | bytes 6291472 | tf_op jit(solution)/shard_map/psum | solution.py:231
  1142.3 5.1 fusion.42
  1147.4 39.5 %all-reduce.14 = (bf16[768]{0:T(1024)(128)(2,1)S(1)}, bf16[768]{0:T(1024)(128)(2,1)S(1)}, bf16[3,192]{1,0:T(4,128)(2,1)S(1)}, bf16[3,3,192]{2,1,0:T(4,128)(2,1)S...) all-reduce(bf16[768]{0:T(1024)(128)(2,1)S(1)} %get-tuple-element.20, ...), channel_id=1, replica_groups=mesh['dp'=8,'mp'=4] {'dp'}, use_global_device_ids=true, to_apply=%region_13.14 | all-reduce | flops 8064 | bytes 32256 | tf_op jit(solution)/shard_map/psum | solution.py:286
  1193.4 12.7 add_add_fusion.2
  1206.1 76.8 %all-reduce.26.cloned.1.call-done = (bf16[768,3,192]{0,2,1:T(8,128)(2,1)}, bf16[192,768]{1,0:T(8,128)(2,1)}, bf16[768,768]{1,0:T(8,128)(2,1)}, bf16[768,768]{1,0:T(8,128)(2,1)}) async-done(((bf16[768,3,192]{0,2,1:T(8,128)(2,1)}, bf16[192,768]{1,0:T(8,128)(2,1)}, bf16[768,768]{1,0:T(8,128)(2,1)}, bf16[768,768]{1,0:T(8,128)(2,1)}), (bf16[768,3,192]{0,2,1:T(8,128)(2,1)}, bf16[192,768]{1,0:T(8,128)(2,1)}, ...) | async-done | bytes 3538960 | tf_op jit(solution)/shard_map/psum | solution.py:288
  (305 shorter events, 155.9 us)
Async XLA Ops:
  7.2 411.7 %copy-start = (bf16[768,768]{1,0:T(8,128)(2,1)S(1)}, bf16[768,768]{1,0:T(8,128)(2,1)}, u32[]{:S(2)}) copy-start(bf16[768,768]{1,0:T(8,128)(2,1)} %param.35) | copy-start | bytes 3538948
  7.2 11.9 copy-start.77
  7.2 12.1 copy-start.53
  7.2 401.1 %all-reduce.22.cloned.1.call-start = ((), (), s32[]{:S(2)}) async-start(), calls=%async_computation.1 | async-start | bytes 6291456 | tf_op jit(solution)/shard_map/psum | solution.py:223
  7.3 49.2 %copy-start.57 = (f32[2048]{0:T(1024)}, f32[2048]{0:T(1024)S(1)}, u32[]{:S(2)}) copy-start(f32[2048]{0:T(1024)S(1)} %iota_convert_fusion) | copy-start | bytes 24580
  9.3 49.7 %copy-start.63 = (f32[2048]{0:T(1024)}, f32[2048]{0:T(1024)S(1)}, u32[]{:S(2)}) copy-start(f32[2048]{0:T(1024)S(1)} %fusion.172) | copy-start | bytes 24580
  10.0 49.0 %copy-start.65 = (f32[2048]{0:T(1024)}, f32[2048]{0:T(1024)S(1)}, u32[]{:S(2)}) copy-start(f32[2048]{0:T(1024)S(1)} %get-tuple-element.97) | copy-start | bytes 24580
  10.0 524.2 %copy-start.45 = (f32[2048]{0:T(1024)}, f32[2048]{0:T(1024)S(1)}, u32[]{:S(2)}) copy-start(f32[2048]{0:T(1024)S(1)} %get-tuple-element.96) | copy-start | bytes 24580
  10.1 273.0 %copy-start.35 = (f32[64,64]{1,0:T(8,128)}, f32[64,64]{1,0:T(8,128)S(1)}, u32[]{:S(2)}) copy-start(f32[64,64]{1,0:T(8,128)S(1)} %get-tuple-element.98) | copy-start | bytes 49156
  10.1 273.0 %copy-start.37 = (f32[64,64]{1,0:T(8,128)}, f32[64,64]{1,0:T(8,128)S(1)}, u32[]{:S(2)}) copy-start(f32[64,64]{1,0:T(8,128)S(1)} %get-tuple-element.99) | copy-start | bytes 49156
  10.9 45.6 %copy-start.78 = (f32[192]{0:T(256)}, f32[192]{0:T(256)S(1)}, u32[]{:S(2)}) copy-start(f32[192]{0:T(256)S(1)} %neg.29) | copy-start | bytes 2308
  13.6 521.9 %copy-start.47 = (f32[2048]{0:T(1024)}, f32[2048]{0:T(1024)S(1)}, u32[]{:S(2)}) copy-start(f32[2048]{0:T(1024)S(1)} %fusion.174) | copy-start | bytes 24580
  16.0 40.5 %copy-start.69 = (f32[768]{0:T(1024)S(1)}, f32[768]{0:T(1024)}, u32[]{:S(2)}) copy-start(f32[768]{0:T(1024)} %param.21) | copy-start | bytes 9220
  16.0 40.5 %copy-start.89 = (bf16[768,3,192]{0,2,1:T(8,128)(2,1)S(1)}, bf16[768,3,192]{0,2,1:T(8,128)(2,1)}, u32[]{:S(2)}) copy-start(bf16[768,3,192]{0,2,1:T(8,128)(2,1)} %param.23) | copy-start | bytes 2654212
  16.0 40.5 %copy-start.93 = (f32[768]{0:T(1024)S(1)}, f32[768]{0:T(1024)}, u32[]{:S(2)}) copy-start(f32[768]{0:T(1024)} %param.22) | copy-start | bytes 9220
  16.0 42.9 %copy-start.43 = (f32[2048]{0:T(1024)}, f32[2048]{0:T(1024)S(1)}, u32[]{:S(2)}) copy-start(f32[2048]{0:T(1024)S(1)} %broadcast_multiply_fusion.5) | copy-start | bytes 24580
  19.0 39.9 %copy-start.61 = (f32[2048]{0:T(1024)}, f32[2048]{0:T(1024)S(1)}, u32[]{:S(2)}) copy-start(f32[2048]{0:T(1024)S(1)} %fusion.43) | copy-start | bytes 24580
  19.1 39.8 %copy-start.54 = (f32[2048]{0:T(1024)}, f32[2048]{0:T(1024)S(1)}, u32[]{:S(2)}) copy-start(f32[2048]{0:T(1024)S(1)} %fusion.175) | copy-start | bytes 24580
  19.1 39.9 %copy-start.71 = (f32[3,192]{1,0:T(4,128)}, f32[3,192]{1,0:T(4,128)S(1)}, u32[]{:S(2)}) copy-start(f32[3,192]{1,0:T(4,128)S(1)} %get-tuple-element.91) | copy-start | bytes 6916
  19.1 39.9 %copy-start.73 = (f32[3,192]{1,0:T(4,128)}, f32[3,192]{1,0:T(4,128)S(1)}, u32[]{:S(2)}) copy-start(f32[3,192]{1,0:T(4,128)S(1)} %get-tuple-element.93) | copy-start | bytes 6916
  19.1 39.9 %copy-start.75 = (f32[3,192]{1,0:T(4,128)}, f32[3,192]{1,0:T(4,128)S(1)}, u32[]{:S(2)}) copy-start(f32[3,192]{1,0:T(4,128)S(1)} %get-tuple-element.92) | copy-start | bytes 6916
  19.2 84.9 %copy-start.39 = (f32[64,64]{0,1:T(8,128)}, f32[64,64]{0,1:T(8,128)S(1)}, u32[]{:S(2)}) copy-start(f32[64,64]{0,1:T(8,128)S(1)} %copy.55) | copy-start | bytes 49156
  19.3 84.8 %copy-start.41 = (f32[64,64]{0,1:T(8,128)}, f32[64,64]{0,1:T(8,128)S(1)}, u32[]{:S(2)}) copy-start(f32[64,64]{0,1:T(8,128)S(1)} %copy.53) | copy-start | bytes 49156
  19.3 37.2 %copy-start.2 = (bf16[2048,768]{1,0:T(8,128)(2,1)S(1)}, bf16[2048,768]{1,0:T(8,128)(2,1)}, u32[]{:S(2)}) copy-start(bf16[2048,768]{1,0:T(8,128)(2,1)} %param.19) | copy-start | bytes 9437188
  320.4 10.4 copy-start.84
  328.1 7.9 copy-start.34
  335.1 73.2 %copy-start.51 = (f32[768]{0:T(1024)S(1)}, f32[768]{0:T(1024)}, u32[]{:S(2)}) copy-start(f32[768]{0:T(1024)} %param.30) | copy-start | bytes 9220
  338.7 76.3 %copy-start.67 = (f32[768]{0:T(1024)S(1)}, f32[768]{0:T(1024)}, u32[]{:S(2)}) copy-start(f32[768]{0:T(1024)} %param.31) | copy-start | bytes 9220
  338.7 76.3 %copy-start.91 = (f32[768]{0:T(1024)S(1)}, f32[768]{0:T(1024)}, u32[]{:S(2)}) copy-start(f32[768]{0:T(1024)} %param.32) | copy-start | bytes 9220
  338.7 173.7 %all-reduce.24.cloned.1.call-start = ((), (), s32[]{:S(2)}) async-start(), calls=%async_computation.2 | async-start | bytes 6291456 | tf_op jit(solution)/shard_map/psum | solution.py:241
  413.0 111.2 %copy-start.49 = (f32[2048]{0:T(1024)}, f32[2048]{0:T(1024)S(1)}, u32[]{:S(2)}) copy-start(f32[2048]{0:T(1024)S(1)} %broadcast_multiply_fusion.4) | copy-start | bytes 24580
  415.0 109.1 %copy-start.59 = (f32[2048]{0:T(1024)}, f32[2048]{0:T(1024)S(1)}, u32[]{:S(2)}) copy-start(f32[2048]{0:T(1024)S(1)} %fusion.176) | copy-start | bytes 24580
  419.0 19.1 %copy-start.30 = (f32[2048,768]{1,0:T(8,128)}, f32[2048,768]{1,0:T(8,128)S(1)}, u32[]{:S(2)}) copy-start(f32[2048,768]{1,0:T(8,128)S(1)} %fusion.278) | copy-start | bytes 18874372
  443.7 570.2 %reduce-scatter.2.cloned.1.call-start = ((), (), s32[]{:S(2)}) async-start(), calls=%async_computation.3 | async-start | bytes 884736 | tf_op jit(solution)/shard_map/reduce_scatter | solution.py:266
  566.0 25.4 %copy-start.10 = (f32[64,960,32]{1,0,2:T(8,128)S(1)}, f32[64,960,32]{1,0,2:T(8,128)}, u32[]{:S(2)}) copy-start(f32[64,960,32]{1,0,2:T(8,128)} %dot_general.142) | copy-start | bytes 23592964
  566.0 25.4 %copy-start.40 = (f32[64,64]{0,1:T(8,128)S(1)}, f32[64,64]{0,1:T(8,128)}, u32[]{:S(2)}) copy-start(f32[64,64]{0,1:T(8,128)} %copy-done.39) | copy-start | bytes 49156
  566.0 25.4 %copy-start.42 = (f32[64,64]{0,1:T(8,128)S(1)}, f32[64,64]{0,1:T(8,128)}, u32[]{:S(2)}) copy-start(f32[64,64]{0,1:T(8,128)} %copy-done.41) | copy-start | bytes 49156
  819.5 31.6 %slice-start.6 = ((s8[6291456]{0:T(1024)(128)(4,1)}), s8[4194304]{0:T(1024)(128)(4,1)S(1)}, s32[]{:S(2)}) async-start(s8[6291456]{0:T(1024)(128)(4,1)} %bitcast.171), calls=%async_computation.12 | async-start | bytes 8388608
  831.9 19.2 %slice-start.7 = ((s8[6291456]{0:T(1024)(128)(4,1)}), s8[2097152]{0:T(1024)(128)(4,1)S(1)}, s32[]{:S(2)}) async-start(s8[6291456]{0:T(1024)(128)(4,1)} %bitcast.171), calls=%async_computation.13 | async-start | bytes 4194304
  851.1 12.5 copy-start.36
  851.2 12.5 copy-start.38
  915.5 7.7 copy-start.17
  936.5 9.5 copy-start.22
  948.5 7.6 copy-start.20
  948.5 7.6 copy-start.46
  948.5 7.6 copy-start.48
  948.5 7.6 copy-start.85
  950.4 185.2 %all-reduce.28.cloned.1.call-start = ((), (), s32[]{:S(2)}) async-start(), calls=%async_computation.5 | async-start | bytes 12582912 | tf_op jit(solution)/shard_map/psum | solution.py:231
  953.3 7.7 slice-start
  974.7 7.0 copy-start.68
  974.7 7.0 copy-start.92
  974.8 308.2 %all-reduce.26.cloned.1.call-start = ((), (), s32[]{:S(2)}) async-start(), calls=%async_computation.4 | async-start | bytes 7077888 | tf_op jit(solution)/shard_map/psum | solution.py:288
  975.0 14.3 %slice-start.2 = ((s8[6291456]{0:T(1024)(128)(4,1)}), s8[4194304]{0:T(1024)(128)(4,1)S(1)}, s32[]{:S(2)}) async-start(s8[6291456]{0:T(1024)(128)(4,1)} %bitcast.169), calls=%async_computation.8 | async-start | bytes 8388608
  981.8 7.6 slice-start.3
  981.8 7.6 copy-start.27
  997.2 145.1 %copy-start.62 = (f32[2048]{0:T(1024)S(1)}, f32[2048]{0:T(1024)}, u32[]{:S(2)}) copy-start(f32[2048]{0:T(1024)} %copy-done.61) | copy-start | bytes 24580
  1138.1 9.3 copy-start.80
  1138.1 9.3 copy-start.81
  1138.1 9.3 copy-start.86
  1138.1 9.3 copy-start.87
  1138.1 55.3 %copy-start.56 = (f32[2048]{0:T(1024)S(1)}, f32[2048]{0:T(1024)}, u32[]{:S(2)}) copy-start(f32[2048]{0:T(1024)} %copy-done.54) | copy-start | bytes 24580
  1138.1 55.3 %copy-start.83 = (f32[768]{0:T(1024)S(1)}, f32[768]{0:T(1024)}, u32[]{:S(2)}) copy-start(f32[768]{0:T(1024)} %param.36) | copy-start | bytes 9220
  1193.4 98.4 %copy-start.1 = (bf16[768,768]{1,0:T(8,128)(2,1)S(1)}, bf16[768,768]{1,0:T(8,128)(2,1)}, u32[]{:S(2)}) copy-start(bf16[768,768]{1,0:T(8,128)(2,1)} %param.35) | copy-start | bytes 3538948
  1282.9 7.3 copy-start.33
  (47 other events, 186.1 us)
Sparse Core Ops, SparseCore 0:
  338.8 69.4 all-reduce.21
  443.8 68.5 all-reduce.23
  950.6 63.2 reduce-scatter.1
  1016.8 118.7 all-reduce.27
  1141.7 141.1 all-reduce.25
where the time goes:
time: 1310 us; the launch traced here: 1300 us
  matrix products  508 us (39%)
  waiting for transfers between devices  338 us (26%)
  local copies, waits for them, and re-layouts  199 us (15%)
  other arithmetic  163 us (12%)
  blocking collectives  73.4 us (6%)
  between operations  16.7 us (1%)
    dot_general x16, matrix products, across(): jnp.einsum('jn,knc->kjc', table, values, precision=lax.Precision.HIGHEST,...  330 us
    psum x1, waiting for transfers between devices, per_device(): lax.psum(down_terms.astype(jnp.bfloat16), 'mp').astype(jnp.float32)  120 us
    dot_general x8, matrix products, exact_product(): jnp.dot(lhs_mat, rhs_mat, precision=lax.Precision.HIGHEST, preferred_elem...  112 us
    psum x1, waiting for transfers between devices, per_device(): lax.psum(grad_proj_in.astype(jnp.bfloat16), 'dp').astype(jnp.float32)  76.8 us
    psum x1, waiting for transfers between devices, per_device(): lax.psum(attn_terms.astype(jnp.bfloat16), 'mp').astype(jnp.float32)  69.5 us
    psum x1, waiting for transfers between devices, per_device(): lax.psum(grad_norm_terms.astype(jnp.bfloat16), 'mp').astype(jnp.float32)  57 us
    psum x1, blocking collectives, per_device(): lax.psum(grad_mix_gain.astype(jnp.bfloat16), 'dp').astype(jnp.float32)  39.5 us
    unnamed x213, local copies, waits for them, and re-layouts  38.2 us
  transfers between devices with their start and end apart: 5, of which 5 were waited for; matrix products, arithmetic and copies ran while one was open for 7% of the time, Pallas kernels for 0%

commit v1 on v0

--- a/solution.py
+++ b/solution.py
@@ -228,7 +228,10 @@
     hidden, gelu_pull = jax.vjp(gelu_exact, pre_act)
     hidden_low = hidden.astype(jnp.bfloat16)
     down_terms = plain_product(hidden_low, proj_down)
-    mlp_out = lax.psum(down_terms.astype(jnp.bfloat16), "mp").astype(jnp.float32) + bias_down
+    mlp_out = (
+        jnp.sum(lax.all_gather(down_terms.astype(jnp.bfloat16), "mp"), axis=0).astype(jnp.float32)
+        + bias_down
+    )
     output = (hidden_one + mlp_out).astype(jnp.bfloat16)
     grad_proj_down = tall_product(hidden_low, cotangent)
     grad_bias_down = jnp.sum(cotangent.astype(jnp.float32), axis=0)

time: 1310 us -> 1360 us (1.038)
  waiting for transfers between devices: 338 us -> 381 us
    psum x1, waiting for transfers between devices: 120 us -> 32.9 us  [per_device(): lax.psum(wide_product(grad_streams_low, proj_flat).astype(jnp.bfloat16),...]
    all_gather x0 -> x1, waiting for transfers between devices: none -> 72.5 us  [per_device(): lax.all_gather(down_terms.astype(jnp.bfloat16), 'mp')]
    psum x1, waiting for transfers between devices: 76.8 us -> 136 us  [per_device(): lax.psum(grad_proj_in.astype(jnp.bfloat16), 'dp').astype(jnp.float32)]
    unnamed x213 -> x207, local copies, waits for them, and re-layouts: 38.2 us -> 42.9 us
  transfers between devices with their start and end apart: 5 -> 6, of which waited for: 5 -> 6; matrix products, arithmetic and copies ran while one was open for 7% -> 6% of each run, Pallas kernels for 0% -> 0%
where the time goes in v1:
time: 1360 us; the launch traced here: 1350 us
  matrix products  512 us (38%)
  waiting for transfers between devices  381 us (28%)
  local copies, waits for them, and re-layouts  204 us (15%)
  other arithmetic  170 us (12%)
  blocking collectives  71 us (5%)
  between operations  16.9 us (1%)
    dot_general x16, matrix products, across(): jnp.einsum('jn,knc->kjc', table, values, precision=lax.Precision.HIGHEST,...  331 us
    psum x1, waiting for transfers between devices, per_device(): lax.psum(grad_proj_in.astype(jnp.bfloat16), 'dp').astype(jnp.float32)  136 us
    dot_general x8, matrix products, exact_product(): jnp.dot(lhs_mat, rhs_mat, precision=lax.Precision.HIGHEST, preferred_elem...  112 us
    all_gather x1, waiting for transfers between devices, per_device(): lax.all_gather(down_terms.astype(jnp.bfloat16), 'mp')  72.5 us
    psum x1, waiting for transfers between devices, per_device(): lax.psum(attn_terms.astype(jnp.bfloat16), 'mp').astype(jnp.float32)  69.5 us
    psum x1, waiting for transfers between devices, per_device(): lax.psum(grad_norm_terms.astype(jnp.bfloat16), 'mp').astype(jnp.float32)  57.5 us
    unnamed x207, local copies, waits for them, and re-layouts  42.9 us
    psum x1, blocking collectives, per_device(): lax.psum(grad_mix_gain.astype(jnp.bfloat16), 'dp').astype(jnp.float32)  37.2 us
  transfers between devices with their start and end apart: 6, of which 6 were waited for; matrix products, arithmetic and copies ran while one was open for 6% of the time, Pallas kernels for 0%

profile of v1, /device:TPU:0, one launch (start us, length us, event | category | flops | bytes accessed | tf_op | source)
XLA Modules:
  0.0 1354.3 jit_solution(7325912070939864586)
XLA Ops:
  19.3 33.9 %all_gather.10 = bf16[2048,192]{0,1:T(8,128)(2,1)S(1)} all-gather(bf16[256,192]{0,1:T(8,128)(2,1)S(1)} %copy-done.53), channel_id=1, replica_groups=mesh['dp'=8,'mp'=4] {'dp'}, dimensions={0}, use_global_device_ids=true | all-gather | bytes 884736 | tf_op jit(solution)/shard_map/all_gather | solution.py:217
  70.7 5.8 copy.51
  76.4 6.4 reshape.291
  82.8 6.4 dot_general.122
  89.2 16.4 %fusion.51 = f32[64,64,576]{2,0,1:T(8,128)} fusion(f32[64,576,32]{1,0,2:T(8,128)} %dot_general.122), kind=kOutput, calls=%fused_computation.95 | convolution fusion | flops 905998336 | bytes 14155776 | tf_op jit(solution)/shard_map/dot_general | solution.py:65
  105.6 20.2 %multiply_add_fusion.1 = (f32[64,64,576]{2,0,1:T(8,128)}, f32[64,64,576]{2,0,1:T(8,128)S(1)}) fusion(f32[64,64,576]{2,0,1:T(8,128)} %fusion.51, f32[64,64]{0,1:T(8,128)S(1)} %copy.55, f32[64,64]{0,1:T(8,128)S(1)} %copy.53, f32[64,576,32]{1,0,2:T(8,128)} %dot_general.122), kind=kOutput, calls=%fused_computation.23 | convolution fusion | flops 922513408 | bytes 33062912 | tf_op jit(solution)/shard_map/dot_general | solution.py:65
  125.8 21.3 %fusion.10 = f32[64,576,64]{1,2,0:T(8,128)} fusion(f32[64,64,576]{2,0,1:T(8,128)S(1)} %get-tuple-element.74), kind=kOutput, calls=%fused_computation.24 | convolution fusion | flops 1811996672 | bytes 18874368 | tf_op jit(solution)/shard_map/jn,knc->kjc/dot_general | solution.py:71
  147.1 21.4 %fusion.12 = f32[64,576,64]{1,2,0:T(8,128)} fusion(f32[64,64,576]{2,0,1:T(8,128)S(1)} %get-tuple-element.74), kind=kOutput, calls=%fused_computation.26 | convolution fusion | flops 1811996672 | bytes 18874368 | tf_op jit(solution)/shard_map/jn,knc->kjc/dot_general | solution.py:71
  168.5 23.3 %subtract_bitcast_fusion.2 = f32[64,64,576]{2,1,0:T(8,128)} fusion(f32[64,576,64]{1,2,0:T(8,128)} %fusion.10, f32[64,64,576]{2,0,1:T(8,128)} %get-tuple-element.73), kind=kOutput, calls=%fused_computation.20 | convolution fusion | flops 1814355968 | bytes 28311552 | tf_op jit(solution)/shard_map/jn,knc->kjc/dot_general | solution.py:71
  191.8 22.7 %add_bitcast_fusion.2 = f32[64,64,576]{2,1,0:T(8,128)S(1)} fusion(f32[64,576,64]{1,2,0:T(8,128)} %fusion.12, f32[64,64,576]{2,0,1:T(8,128)} %get-tuple-element.73), kind=kOutput, calls=%fused_computation.21 | convolution fusion | flops 1814355968 | bytes 28311552 | tf_op jit(solution)/shard_map/jn,knc->kjc/dot_general | solution.py:71
  218.6 4.5 tile.16
  223.2 10.7 tile.17
  240.6 10.9 tile.19
  251.4 9.5 multiply_subtract_fusion.5
  261.0 7.9 fusion.93
  268.9 7.8 fusion.105
  276.6 7.9 fusion.95
  284.5 14.9 %multiply_add_fusion.4 = (f32[64,384,64]{1,2,0:T(8,128)}, f32[64,384,64]{1,2,0:T(8,128)}) fusion(f32[64,64]{1,0:T(8,128)S(1)} %get-tuple-element.95, f32[64,64]{1,0:T(8,128)S(1)} %get-tuple-element.96, f32[64,384,64]{1,2,0:T(8,128)} %fusion.93, f32[64,384,64]{1,2,0:T(8,128)} %fusion.105, f32[64,384,64]{1,2,0:T(8,128)} %fusion.95, ...), kind=kOutput, calls=%fused_computation.90 | convolution fusion | flops 1220599808 | bytes 37781504 | tf_op jit(solution)/shard_map/jn,knc->kjc/dot_general | solution.py:71
  299.5 6.5 copy.80
  313.1 5.7 fusion.1
  322.1 4.9 fusion.291
  340.4 69.5 %all-reduce.21.cloned.1.call-done = bf16[2048,768]{1,0:T(8,128)(2,1)} async-done(((bf16[2048,768]{1,0:T(8,128)(2,1)}), bf16[2048,768]{1,0:T(8,128)(2,1)}) %all-reduce.21.cloned.1.call-update) | async-done | bytes 3145744 | tf_op jit(solution)/shard_map/psum | solution.py:223
  420.5 19.1 %fusion.283 = (bf16[768]{0:T(1024)(128)(2,1)}, bf16[2048,768]{1,0:T(8,128)(2,1)S(1)}, f32[2048,768]{1,0:T(8,128)}) fusion(f32[2048,768]{1,0:T(8,128)S(1)} %fusion.278, f32[768]{0:T(1024)S(1)} %copy-done.82, bf16[2048,768]{1,0:T(8,128)(2,1)S(1)} %copy-done.22, bf16[768,768]{1,0:T(8,128)(2,1)S(1)} %copy-done), kind=kOutput, calls=%fused_computation.369 | convolution fusion | flops 2532310272 | bytes 20058624 | tf_op jit(solution)/shard_map/dot_general | solution.py:59
  445.3 5.5 multiply_convert_fusion
  456.5 57.5 %all-reduce.23.cloned.1.call-done = bf16[2048,768]{1,0:T(8,128)(2,1)} async-done(((bf16[2048,768]{1,0:T(8,128)(2,1)}), bf16[2048,768]{1,0:T(8,128)(2,1)}) %all-reduce.23.cloned.1.call-update) | async-done | bytes 3145744 | tf_op jit(solution)/shard_map/psum | solution.py:244
  513.9 5.2 fusion.40
  519.1 6.7 fusion.41
  525.8 72.5 %all-gather.3.cloned.1.call-done = bf16[8192,768]{1,0:T(8,128)(2,1)} async-done(((bf16[2048,768]{1,0:T(8,128)(2,1)}), bf16[8192,768]{1,0:T(8,128)(2,1)}) %all-gather.3.cloned.1.call-update) | async-done | bytes 12582928 | tf_op jit(solution)/shard_map/all_gather | solution.py:232
  598.3 9.0 reduce_sum.231
  607.3 10.2 fusion.285
  617.5 5.6 multiply_reduce_fusion.4
  627.8 9.1 copy.62
  636.9 9.0 reshape.294
  645.9 8.9 dot_general.142
  654.8 25.8 %fusion.30 = f32[64,64,960]{2,0,1:T(8,128)} fusion(f32[64,960,32]{1,0,2:T(8,128)} %dot_general.142), kind=kOutput, calls=%fused_computation.46 | convolution fusion | flops 1509978112 | bytes 23592960 | tf_op jit(solution)/shard_map/dot_general | solution.py:65
  680.7 26.3 %multiply_add_fusion = (f32[64,64,960]{2,0,1:T(8,128)}, f32[64,64,960]{2,0,1:T(8,128)}) fusion(f32[64,64,960]{2,0,1:T(8,128)} %fusion.30, f32[64,64]{0,1:T(8,128)S(1)} %copy-done.40, f32[64,64]{0,1:T(8,128)S(1)} %copy-done.42, f32[64,960,32]{1,0,2:T(8,128)S(1)} %copy-done.8), kind=kOutput, calls=%fused_computation.7 | convolution fusion | flops 1537503232 | bytes 55083008 | tf_op jit(solution)/shard_map/dot_general | solution.py:65
  707.0 36.1 %fusion.2 = f32[64,960,64]{1,2,0:T(8,128)} fusion(f32[64,64,960]{2,0,1:T(8,128)} %get-tuple-element.66), kind=kOutput, calls=%fused_computation.8 | convolution fusion | flops 3019956224 | bytes 31457280 | tf_op jit(solution)/shard_map/jn,knc->kjc/dot_general | solution.py:71
  743.1 36.3 %fusion.4 = f32[64,960,64]{1,2,0:T(8,128)} fusion(f32[64,64,960]{2,0,1:T(8,128)} %get-tuple-element.66), kind=kOutput, calls=%fused_computation.10 | convolution fusion | flops 3019956224 | bytes 31457280 | tf_op jit(solution)/shard_map/jn,knc->kjc/dot_general | solution.py:71
  779.4 32.7 %subtract_bitcast_fusion = f32[64,64,960]{2,1,0:T(8,128)} fusion(f32[64,960,64]{1,2,0:T(8,128)} %fusion.2, f32[64,64,960]{2,0,1:T(8,128)} %get-tuple-element.65), kind=kOutput, calls=%fused_computation.4 | convolution fusion | flops 3023888384 | bytes 47185920 | tf_op jit(solution)/shard_map/jn,knc->kjc/dot_general | solution.py:71
  812.1 32.7 %add_bitcast_fusion = f32[64,64,960]{2,1,0:T(8,128)} fusion(f32[64,960,64]{1,2,0:T(8,128)} %fusion.4, f32[64,64,960]{2,0,1:T(8,128)} %get-tuple-element.65), kind=kOutput, calls=%fused_computation.5 | convolution fusion | flops 3023888384 | bytes 47185920 | tf_op jit(solution)/shard_map/jn,knc->kjc/dot_general | solution.py:71
  851.5 10.7 tile.41
  868.8 10.8 tile.43
  879.6 22.7 %multiply_add_fusion.3 = (f32[64,64,384]{2,1,0:T(8,128)}, f32[64,64,384]{2,1,0:T(8,128)}, f32[64,64,384]{2,1,0:T(8,128)}, f32[64,64,384]{2,1,0:T(8,128)}) fusion(f32[64,64,384]{2,1,0:T(8,128)} %tile.43, f32[64,64,384]{2,1,0:T(8,128)} %tile.41, f32[64,64,960]{2,1,0:T(8,128)} %subtract_bitcast_fusion, f32[64,64,960]{2,1,0:T(8,128)} %add_bitcast_fusion), kind=kLoop, calls=%fused_computation.71 | loop fusion | flops 18874368 | bytes 62914560 | tf_op jit(solution)/shard_map/add | solution.py:168
  902.3 4.7 slice_add_fusion
  907.5 12.5 fusion.26
  920.0 12.7 fusion.27
  932.7 4.6 slice_add_fusion.1
  939.3 12.6 fusion.28
  952.0 28.1 %add_bitcast_fusion.1 = (f32[64,64,576]{2,1,0:T(8,128)}, f32[64,64,576]{2,1,0:T(8,128)}) fusion(f32[64,64]{1,0:T(8,128)S(1)} %copy-done.36, f32[64,64]{1,0:T(8,128)S(1)} %copy-done.38, f32[64,576,64]{1,2,0:T(8,128)} %fusion.26, f32[64,576,64]{1,2,0:T(8,128)} %fusion.28, f32[64,576,64]{1,2,0:T(8,128)} %fusion.27, f32[64,64,192]{2,1,0:T(8,128)} %copy-done.14, ...), kind=kOutput, calls=%fused_computation.18 | convolution fusion | flops 1833230336 | bytes 56655872 | tf_op jit(solution)/shard_map/jn,knc->kjc/dot_general | solution.py:71
  980.1 11.9 reshape.296
  992.0 11.9 reshape.295
  1003.9 7.7 fusion.160
  1011.6 6.7 fusion
  1018.3 6.6 div.72
  1024.9 6.5 fusion.290
  1042.0 5.3 multiply_reduce_fusion.3
  1057.3 8.5 convolution_convert_fusion.4
  1073.4 6.8 convolution_convert_fusion.3
  1092.9 32.9 %all-reduce.25.cloned.1.call-done = bf16[2048,768]{1,0:T(8,128)(2,1)} async-done(((bf16[2048,768]{1,0:T(8,128)(2,1)}), bf16[2048,768]{1,0:T(8,128)(2,1)}) %all-reduce.25.cloned.1.call-update) | async-done | bytes 3145744 | tf_op jit(solution)/shard_map/psum | solution.py:264
  1132.1 5.1 fusion.42
  1137.2 37.2 %all-reduce.14 = (bf16[768]{0:T(1024)(128)(2,1)S(1)}, bf16[768]{0:T(1024)(128)(2,1)S(1)}, bf16[3,192]{1,0:T(4,128)(2,1)S(1)}, bf16[3,3,192]{2,1,0:T(4,128)(2,1)S...) all-reduce(bf16[768]{0:T(1024)(128)(2,1)S(1)} %get-tuple-element.20, ...), channel_id=1, replica_groups=mesh['dp'=8,'mp'=4] {'dp'}, use_global_device_ids=true, to_apply=%region_13.14 | all-reduce | flops 8064 | bytes 32256 | tf_op jit(solution)/shard_map/psum | solution.py:289
  1180.9 12.0 reduce-scatter.2.cloned.1.call-done
  1194.4 7.5 add_add_fusion.2
  1202.0 136.4 %all-reduce.27.cloned.1.call-done = (bf16[768,3,192]{0,2,1:T(8,128)(2,1)}, bf16[192,768]{1,0:T(8,128)(2,1)}, bf16[768,768]{1,0:T(8,128)(2,1)}, bf16[768,768]{1,0:T(8,128)(2,1)}) async-done(((bf16[768,3,192]{0,2,1:T(8,128)(2,1)}, bf16[192,768]{1,0:T(8,128)(2,1)}, bf16[768,768]{1,0:T(8,128)(2,1)}, bf16[768,768]{1,0:T(8,128)(2,1)}), (bf16[768,3,192]{0,2,1:T(8,128)(2,1)}, bf16[192,768]{1,0:T(8,128)(2,1)}, ...) | async-done | bytes 3538960 | tf_op jit(solution)/shard_map/psum | solution.py:291
  (302 shorter events, 168.6 us)
Async XLA Ops:
  7.2 413.3 %copy-start = (bf16[768,768]{1,0:T(8,128)(2,1)S(1)}, bf16[768,768]{1,0:T(8,128)(2,1)}, u32[]{:S(2)}) copy-start(bf16[768,768]{1,0:T(8,128)(2,1)} %param.35) | copy-start | bytes 3538948
  7.2 11.9 copy-start.77
  7.2 12.1 copy-start.53
  7.2 402.7 %all-reduce.21.cloned.1.call-start = ((), (), s32[]{:S(2)}) async-start(), calls=%async_computation.1 | async-start | bytes 6291456 | tf_op jit(solution)/shard_map/psum | solution.py:223
  7.3 49.2 %copy-start.58 = (f32[2048]{0:T(1024)}, f32[2048]{0:T(1024)S(1)}, u32[]{:S(2)}) copy-start(f32[2048]{0:T(1024)S(1)} %iota_convert_fusion) | copy-start | bytes 24580
  9.3 49.6 %copy-start.62 = (f32[2048]{0:T(1024)}, f32[2048]{0:T(1024)S(1)}, u32[]{:S(2)}) copy-start(f32[2048]{0:T(1024)S(1)} %fusion.172) | copy-start | bytes 24580
  10.0 49.0 %copy-start.64 = (f32[2048]{0:T(1024)}, f32[2048]{0:T(1024)S(1)}, u32[]{:S(2)}) copy-start(f32[2048]{0:T(1024)S(1)} %get-tuple-element.94) | copy-start | bytes 24580
  10.0 613.1 %copy-start.47 = (f32[2048]{0:T(1024)}, f32[2048]{0:T(1024)S(1)}, u32[]{:S(2)}) copy-start(f32[2048]{0:T(1024)S(1)} %get-tuple-element.93) | copy-start | bytes 24580
  10.1 274.4 %copy-start.35 = (f32[64,64]{1,0:T(8,128)}, f32[64,64]{1,0:T(8,128)S(1)}, u32[]{:S(2)}) copy-start(f32[64,64]{1,0:T(8,128)S(1)} %get-tuple-element.95) | copy-start | bytes 49156
  10.1 274.4 %copy-start.37 = (f32[64,64]{1,0:T(8,128)}, f32[64,64]{1,0:T(8,128)S(1)}, u32[]{:S(2)}) copy-start(f32[64,64]{1,0:T(8,128)S(1)} %get-tuple-element.96) | copy-start | bytes 49156
  10.9 45.7 %copy-start.78 = (f32[192]{0:T(256)}, f32[192]{0:T(256)S(1)}, u32[]{:S(2)}) copy-start(f32[192]{0:T(256)S(1)} %neg.29) | copy-start | bytes 2308
  13.6 610.9 %copy-start.49 = (f32[2048]{0:T(1024)}, f32[2048]{0:T(1024)S(1)}, u32[]{:S(2)}) copy-start(f32[2048]{0:T(1024)S(1)} %fusion.174) | copy-start | bytes 24580
  16.0 40.6 %copy-start.74 = (f32[768]{0:T(1024)S(1)}, f32[768]{0:T(1024)}, u32[]{:S(2)}) copy-start(f32[768]{0:T(1024)} %param.21) | copy-start | bytes 9220
  16.0 40.5 %copy-start.89 = (bf16[768,3,192]{0,2,1:T(8,128)(2,1)S(1)}, bf16[768,3,192]{0,2,1:T(8,128)(2,1)}, u32[]{:S(2)}) copy-start(bf16[768,3,192]{0,2,1:T(8,128)(2,1)} %param.23) | copy-start | bytes 2654212
  16.0 40.5 %copy-start.93 = (f32[768]{0:T(1024)S(1)}, f32[768]{0:T(1024)}, u32[]{:S(2)}) copy-start(f32[768]{0:T(1024)} %param.22) | copy-start | bytes 9220
  16.0 42.9 %copy-start.45 = (f32[2048]{0:T(1024)}, f32[2048]{0:T(1024)S(1)}, u32[]{:S(2)}) copy-start(f32[2048]{0:T(1024)S(1)} %broadcast_multiply_fusion.5) | copy-start | bytes 24580
  19.0 39.8 %copy-start.60 = (f32[2048]{0:T(1024)}, f32[2048]{0:T(1024)S(1)}, u32[]{:S(2)}) copy-start(f32[2048]{0:T(1024)S(1)} %fusion.43) | copy-start | bytes 24580
  19.1 39.8 %copy-start.56 = (f32[2048]{0:T(1024)}, f32[2048]{0:T(1024)S(1)}, u32[]{:S(2)}) copy-start(f32[2048]{0:T(1024)S(1)} %fusion.175) | copy-start | bytes 24580
  19.1 39.8 %copy-start.68 = (f32[3,192]{1,0:T(4,128)}, f32[3,192]{1,0:T(4,128)S(1)}, u32[]{:S(2)}) copy-start(f32[3,192]{1,0:T(4,128)S(1)} %get-tuple-element.88) | copy-start | bytes 6916
  19.1 39.8 %copy-start.70 = (f32[3,192]{1,0:T(4,128)}, f32[3,192]{1,0:T(4,128)S(1)}, u32[]{:S(2)}) copy-start(f32[3,192]{1,0:T(4,128)S(1)} %get-tuple-element.90) | copy-start | bytes 6916
  19.1 39.8 %copy-start.72 = (f32[3,192]{1,0:T(4,128)}, f32[3,192]{1,0:T(4,128)S(1)}, u32[]{:S(2)}) copy-start(f32[3,192]{1,0:T(4,128)S(1)} %get-tuple-element.89) | copy-start | bytes 6916
  19.2 86.4 %copy-start.39 = (f32[64,64]{0,1:T(8,128)}, f32[64,64]{0,1:T(8,128)S(1)}, u32[]{:S(2)}) copy-start(f32[64,64]{0,1:T(8,128)S(1)} %copy.55) | copy-start | bytes 49156
  19.3 86.3 %copy-start.41 = (f32[64,64]{0,1:T(8,128)}, f32[64,64]{0,1:T(8,128)S(1)}, u32[]{:S(2)}) copy-start(f32[64,64]{0,1:T(8,128)S(1)} %copy.53) | copy-start | bytes 49156
  19.3 37.2 %copy-start.2 = (bf16[2048,768]{1,0:T(8,128)(2,1)S(1)}, bf16[2048,768]{1,0:T(8,128)(2,1)}, u32[]{:S(2)}) copy-start(bf16[2048,768]{1,0:T(8,128)(2,1)} %param.19) | copy-start | bytes 9437188
  322.1 10.4 copy-start.84
  329.7 7.9 copy-start.34
  336.7 73.2 %copy-start.51 = (f32[768]{0:T(1024)S(1)}, f32[768]{0:T(1024)}, u32[]{:S(2)}) copy-start(f32[768]{0:T(1024)} %param.30) | copy-start | bytes 9220
  340.3 76.2 %copy-start.66 = (f32[768]{0:T(1024)S(1)}, f32[768]{0:T(1024)}, u32[]{:S(2)}) copy-start(f32[768]{0:T(1024)} %param.31) | copy-start | bytes 9220
  340.3 76.2 %copy-start.91 = (f32[768]{0:T(1024)S(1)}, f32[768]{0:T(1024)}, u32[]{:S(2)}) copy-start(f32[768]{0:T(1024)} %param.32) | copy-start | bytes 9220
  340.3 173.6 %all-reduce.23.cloned.1.call-start = ((), (), s32[]{:S(2)}) async-start(), calls=%async_computation.2 | async-start | bytes 6291456 | tf_op jit(solution)/shard_map/psum | solution.py:244
  414.6 192.7 %copy-start.43 = (f32[2048]{0:T(1024)}, f32[2048]{0:T(1024)S(1)}, u32[]{:S(2)}) copy-start(f32[2048]{0:T(1024)S(1)} %broadcast_multiply_fusion.4) | copy-start | bytes 24580
  416.6 190.7 %copy-start.54 = (f32[2048]{0:T(1024)}, f32[2048]{0:T(1024)S(1)}, u32[]{:S(2)}) copy-start(f32[2048]{0:T(1024)S(1)} %fusion.176) | copy-start | bytes 24580
  420.5 19.1 %copy-start.28 = (f32[2048,768]{1,0:T(8,128)}, f32[2048,768]{1,0:T(8,128)S(1)}, u32[]{:S(2)}) copy-start(f32[2048,768]{1,0:T(8,128)S(1)} %fusion.278) | copy-start | bytes 18874372
  445.2 153.1 %all-gather.3.cloned.1.call-start = ((), (), s32[]{:S(2)}) async-start(), calls=%async_computation.5 | async-start | bytes 15728640 | tf_op jit(solution)/shard_map/all_gather | solution.py:232
  456.4 669.4 %all-reduce.25.cloned.1.call-start = ((), (), s32[]{:S(2)}) async-start(), calls=%async_computation.3 | async-start | bytes 6291456 | tf_op jit(solution)/shard_map/psum | solution.py:264
  598.3 9.0 copy-start.83
  607.3 10.2 copy-start.29
  654.8 25.8 %copy-start.8 = (f32[64,960,32]{1,0,2:T(8,128)S(1)}, f32[64,960,32]{1,0,2:T(8,128)}, u32[]{:S(2)}) copy-start(f32[64,960,32]{1,0,2:T(8,128)} %dot_general.142) | copy-start | bytes 23592964
  654.8 25.8 %copy-start.40 = (f32[64,64]{0,1:T(8,128)S(1)}, f32[64,64]{0,1:T(8,128)}, u32[]{:S(2)}) copy-start(f32[64,64]{0,1:T(8,128)} %copy-done.39) | copy-start | bytes 49156
  654.8 25.8 %copy-start.42 = (f32[64,64]{0,1:T(8,128)S(1)}, f32[64,64]{0,1:T(8,128)}, u32[]{:S(2)}) copy-start(f32[64,64]{0,1:T(8,128)} %copy-done.41) | copy-start | bytes 49156
  907.5 31.8 %slice-start.4 = ((s8[6291456]{0:T(1024)(128)(4,1)}), s8[4194304]{0:T(1024)(128)(4,1)S(1)}, s32[]{:S(2)}) async-start(s8[6291456]{0:T(1024)(128)(4,1)} %bitcast.170), calls=%async_computation.11 | async-start | bytes 8388608
  920.0 19.3 %slice-start.5 = ((s8[6291456]{0:T(1024)(128)(4,1)}), s8[2097152]{0:T(1024)(128)(4,1)S(1)}, s32[]{:S(2)}) async-start(s8[6291456]{0:T(1024)(128)(4,1)} %bitcast.170), calls=%async_computation.12 | async-start | bytes 4194304
  939.3 12.6 copy-start.36
  939.3 12.6 copy-start.38
  1003.9 7.7 copy-start.15
  1034.3 7.6 slice-start
  1057.2 11.5 copy-start.20
  1057.2 135.7 %reduce-scatter.2.cloned.1.call-start = ((), (), s32[]{:S(2)}) async-start(), calls=%async_computation.4 | async-start | bytes 884736 | tf_op jit(solution)/shard_map/reduce_scatter | solution.py:269
  1071.1 9.0 copy-start.24
  1073.1 11.4 copy-start.32
  1073.1 11.4 copy-start.46
  1073.1 11.4 copy-start.57
  1073.1 11.4 copy-start.75
  1073.1 11.4 copy-start.94
  1073.1 265.3 %all-reduce.27.cloned.1.call-start = ((), (), s32[]{:S(2)}) async-start(), calls=%async_computation.6 | async-start | bytes 7077888 | tf_op jit(solution)/shard_map/psum | solution.py:291
  1073.4 11.2 copy-start.4
  1090.4 41.7 %copy-start.61 = (f32[2048]{0:T(1024)S(1)}, f32[2048]{0:T(1024)}, u32[]{:S(2)}) copy-start(f32[2048]{0:T(1024)} %copy-done.60) | copy-start | bytes 24580
  1128.2 9.0 copy-start.80
  1128.2 9.0 copy-start.81
  1128.2 9.0 copy-start.86
  1128.2 9.0 copy-start.87
  1128.2 66.2 %copy-start.76 = (f32[768]{0:T(1024)S(1)}, f32[768]{0:T(1024)}, u32[]{:S(2)}) copy-start(f32[768]{0:T(1024)} %param.21) | copy-start | bytes 9220
  1194.4 152.8 %copy-start.1 = (bf16[768,768]{1,0:T(8,128)(2,1)S(1)}, bf16[768,768]{1,0:T(8,128)(2,1)}, u32[]{:S(2)}) copy-start(bf16[768,768]{1,0:T(8,128)(2,1)} %param.35) | copy-start | bytes 3538948
  1338.4 7.3 copy-start.33
  (45 other events, 172.8 us)
Sparse Core Ops, SparseCore 0:
  340.4 69.4 all-reduce.20
  445.3 68.5 all-reduce.22
  516.1 82.2 all-gather.2
  1057.3 68.4 all-reduce.24
  1129.5 63.2 reduce-scatter.1
  1198.9 139.4 all-reduce.26
